TPU v7x, 128 devices: a whole 4x4x4 slice. The times are simulated.
128 devices in a mesh: grp: 2 (over z_hi), wid: 8 (over y, core), hid: 8 (over z_lo, x).
Axes of the slice: x: 4, y: 4, z: 4 (z_hi: 2, z_lo: 2; z = z_hi * 2 + z_lo), core: 2. Of those that a mesh axis runs over, the one named last changes fastest.
Arguments:
- student_in: bfloat16 [1024, 4096], P('wid'), may hold values from -6 to 6
- norm_gain: float32 [4096], replicated, may hold values from 0.1 to 1.9
- gate_weight: bfloat16 [4096, 7168], P(None, ('grp', 'hid')), may hold values from -0.09375 to 0.09375
- up_weight: bfloat16 [4096, 7168], P(None, ('grp', 'hid')), may hold values from -0.09375 to 0.09375
- down_weight: bfloat16 [7168, 4096], P(('grp', 'hid')), may hold values from -0.0625 to 0.0625
- projection: bfloat16 [4096, 8, 1024], P(None, None, ('grp', 'hid')), may hold values from -0.09375 to 0.09375
- teacher_in: bfloat16 [1024, 8192], P(None, 'wid'), may hold values from -6 to 6
- teacher_gate: bfloat16 [8192, 14336], P('wid', ('grp', 'hid')), may hold values from -0.0625 to 0.0625
- teacher_up: bfloat16 [8192, 14336], P('wid', ('grp', 'hid')), may hold values from -0.0625 to 0.0625
- teacher_down: bfloat16 [14336, 8192], P(('grp', 'hid'), 'wid'), may hold values from -0.046875 to 0.046875
Outputs:
- grad_gate: bfloat16 [4096, 7168], P('wid', ('grp', 'hid'))
- grad_up: bfloat16 [4096, 7168], P('wid', ('grp', 'hid'))
- grad_down: bfloat16 [7168, 4096], P(('grp', 'hid'), 'wid')
- grad_proj: bfloat16 [4096, 8, 1024], P('wid', None, ('grp', 'hid'))
- input_grad: float32 [1024, 4096], P('wid', ('grp', 'hid'))
All inputs are finite; a program needn't handle non-finite values.
Results may differ from a plain program's by a relative error of at most 0.02.
Values may be sent and summed in bfloat16 or wider, within the bound.
A program may use at most 128 MiB of HBM per device.

v0:
```python
import math
import jax
import jax.numpy as jnp
from jax import lax
from jax.sharding import Mesh
from jax.sharding import PartitionSpec as P

WID = ("wid_0", "wid_1")
GRP_HID = ("grp", "hid_0", "hid_1")


def split_up(array, dim, peers):
    shape = array.shape
    blocks = array.reshape(*shape[:dim], peers, shape[dim] // peers, *shape[dim + 1 :])
    return jnp.moveaxis(blocks, dim, 0)


def one_scatter(arrays, axis, dims):
    peers = lax.axis_size(axis)
    blocks = [split_up(a, dim, peers) for a, dim in zip(arrays, dims)]
    lines = jnp.concatenate([b.reshape(peers, -1) for b in blocks], axis=1)
    rows = max(16, -(-lines.shape[1] // 1024) * 8)
    lines = jnp.pad(lines, ((0, 0), (0, rows * 128 - lines.shape[1]))).reshape(-1, 128)
    vector, at, done = (lax.psum_scatter(lines, axis, tiled=True).reshape(-1), 0, [])
    for b in blocks:
        part = b[0]
        done.append(vector[at : at + part.size].reshape(part.shape))
        at += part.size
    return tuple(done)


def from_everyone(array, axis):
    peers = lax.axis_size(axis)
    return lax.all_to_all(
        jnp.broadcast_to(array[None], (peers, *array.shape)), axis, 0, 0, tiled=True
    )


def joined_along(blocks, dim):
    blocks = jnp.moveaxis(blocks, 0, dim)
    shape = blocks.shape
    return blocks.reshape(*shape[:dim], shape[dim] * shape[dim + 1], *shape[dim + 2 :])


def whole_of(array, axes, dim):
    far, near = axes
    blocks = from_everyone(from_everyone(array, far), near)
    return joined_along(blocks.swapaxes(0, 1).reshape(-1, *array.shape), dim)


def sent_and_summed(array, axis, dim):
    blocks = split_up(array, dim, lax.axis_size(axis))
    arrived = lax.all_to_all(blocks, axis, split_axis=0, concat_axis=0, tiled=True)
    return arrived.astype(jnp.float32).sum(axis=0)


def summed_rows(array, axes, dim):
    far, near = axes
    blocks = split_up(array, dim, lax.axis_size(far))
    nearer = sent_and_summed(blocks, near, dim + 1)
    arrived = lax.all_to_all(
        nearer.astype(jnp.bfloat16), far, split_axis=0, concat_axis=0, tiled=True
    )
    return arrived.astype(jnp.float32).sum(axis=0)


def rows_for(lines, peers):
    spare = -len(lines) % peers
    return jnp.pad(lines, [(0, spare)] + [(0, 0)] * (lines.ndim - 1))


def total_of(array, axes):
    lines = array.reshape(-1, array.shape[-1])
    own = summed_rows(rows_for(lines, lax.axis_size(axes[0]) * lax.axis_size(axes[1])), axes, 0)
    whole = whole_of(own.astype(jnp.bfloat16), axes, 0)
    return whole[: len(lines)].reshape(array.shape).astype(jnp.float32)


def of_everyone(array, axis):
    everything = from_everyone(array, axis)
    return jnp.sum(everything, axis=0)


def in_one_piece(arrays, axis, dim, along):
    ends, at = ([], 0)
    for a in arrays[:-1]:
        at += a.shape[along]
        ends.append(at)
    both = jnp.concatenate(arrays, axis=along)
    return tuple(jnp.split(lax.all_gather(both, axis, axis=dim, tiled=True), ends, axis=along))


def shards(
    student_in,
    norm_gain,
    gate_weight,
    up_weight,
    down_weight,
    projection,
    teacher_in,
    teacher_gate,
    teacher_up,
    teacher_down,
):
    f32 = jnp.float32
    bf16 = jnp.bfloat16
    gate_part = jnp.dot(teacher_in, teacher_gate, preferred_element_type=f32)
    up_part = jnp.dot(teacher_in, teacher_up, preferred_element_type=f32)
    gate_rows, up_rows = tuple(
        (
            part.astype(jnp.float32)
            for part in one_scatter(
                (gate_part.astype(jnp.bfloat16), up_part.astype(jnp.bfloat16)), WID, (0, 0)
            )
        )
    )
    teacher_hidden = (gate_rows * jax.nn.sigmoid(gate_rows) * up_rows).astype(bf16)
    feature_part = jnp.dot(
        whole_of(teacher_hidden, ("wid_0", "wid_1"), 0), teacher_down, preferred_element_type=f32
    )
    target_cols = (
        lax.psum_scatter(
            feature_part.astype(jnp.bfloat16), GRP_HID, scatter_dimension=1, tiled=True
        )
        .astype(jnp.float32)
        .astype(bf16)
    )
    target = lax.all_to_all(target_cols, WID, split_axis=0, concat_axis=1, tiled=True)
    tokens_dev = student_in.shape[0]
    width = student_in.shape[1]
    total_tokens = tokens_dev * lax.axis_size(WID)
    inputs = student_in.astype(f32)
    inverse_rms = lax.rsqrt(jnp.mean(inputs * inputs, axis=-1, keepdims=True) + 1e-05)
    normed = (inputs * inverse_rms * norm_gain).astype(bf16)
    gate_sum = jnp.dot(normed, gate_weight, preferred_element_type=f32)
    up_sum = jnp.dot(normed, up_weight, preferred_element_type=f32)
    sigma = jax.nn.sigmoid(gate_sum)
    hidden = (gate_sum * sigma * up_sum).astype(bf16)
    branch = total_of(
        jnp.dot(hidden, down_weight, preferred_element_type=f32).astype(jnp.bfloat16),
        ("grp", ("hid_0", "hid_1")),
    )
    summed = (inputs + branch).astype(bf16)
    proj_local = projection.reshape(width, -1)
    features = jnp.dot(summed, proj_local, preferred_element_type=f32)
    feature_error = ((features - target.astype(f32)) / math.sqrt(total_tokens)).astype(bf16)
    feature_grad = total_of(
        jnp.dot(feature_error, proj_local.T, preferred_element_type=f32).astype(jnp.bfloat16),
        ("grp", ("hid_0", "hid_1")),
    )
    branch_grad = feature_grad.astype(bf16)
    hidden_grad = jnp.dot(branch_grad, down_weight.T, preferred_element_type=f32)
    gate_grad = (hidden_grad * up_sum * sigma * (1.0 + gate_sum * (1.0 - sigma))).astype(bf16)
    up_grad = (hidden_grad * gate_sum * sigma).astype(bf16)
    normed_grad = jnp.dot(gate_grad, gate_weight.T, preferred_element_type=f32) + jnp.dot(
        up_grad, up_weight.T, preferred_element_type=f32
    )
    share_cols = width // lax.axis_size(GRP_HID)
    offset = lax.axis_index(GRP_HID) * share_cols
    normed_share = sent_and_summed(normed_grad.astype(jnp.bfloat16), GRP_HID, 1)
    input_share = lax.dynamic_slice_in_dim(inputs, offset, share_cols, 1)
    gain_share = lax.dynamic_slice_in_dim(norm_gain, offset, share_cols, 0)
    scaled = normed_share * gain_share
    moment = of_everyone(jnp.sum(scaled * input_share, axis=-1, keepdims=True), GRP_HID) / width
    grad_share = lax.dynamic_slice_in_dim(feature_grad, offset, share_cols, 1)
    input_grad = grad_share + inverse_rms * (
        scaled - input_share * inverse_rms * inverse_rms * moment
    )
    paired_grad = jnp.concatenate([gate_grad, up_grad], axis=1)
    summed_cols, branch_cols = (
        lax.all_to_all(summed, WID, split_axis=1, concat_axis=0, tiled=True),
        lax.all_to_all(branch_grad, WID, split_axis=1, concat_axis=0, tiled=True),
    )
    hidden_all, error_all = in_one_piece((hidden, feature_error), WID, 0, 1)
    weight_grad = lax.psum_scatter(
        jnp.dot(normed.T, paired_grad, preferred_element_type=f32).astype(jnp.bfloat16),
        WID,
        scatter_dimension=0,
        tiled=True,
    ).astype(jnp.float32)
    hidden_cols = gate_grad.shape[1]
    grad_gate = weight_grad[:, :hidden_cols].astype(bf16)
    grad_up = weight_grad[:, hidden_cols:].astype(bf16)
    grad_down = jnp.dot(hidden_all.T, branch_cols, preferred_element_type=f32).astype(bf16)
    grad_proj = jnp.dot(summed_cols.T, error_all, preferred_element_type=f32).astype(bf16)
    grad_proj = grad_proj.reshape(summed_cols.shape[1], lax.axis_size(WID), -1)
    return (grad_gate, grad_up, grad_down, grad_proj, input_grad)


def solution(mesh):
    split = Mesh(
        mesh.devices.reshape(mesh.shape["grp"], 4, 2, 2, 4),
        ("grp", "wid_0", "wid_1", "hid_0", "hid_1"),
    )
    in_specs = (
        P(WID, None),
        P(),
        P(None, GRP_HID),
        P(None, GRP_HID),
        P(GRP_HID, None),
        P(None, None, GRP_HID),
        P(None, WID),
        P(WID, GRP_HID),
        P(WID, GRP_HID),
        P(GRP_HID, WID),
    )
    out_specs = (
        P(WID, GRP_HID),
        P(WID, GRP_HID),
        P(GRP_HID, WID),
        P(WID, None, GRP_HID),
        P(WID, GRP_HID),
    )
    return jax.shard_map(
        shards, mesh=split, in_specs=in_specs, out_specs=out_specs, check_vma=False
    )
```

profile of v0, /device:TPU:1, one launch (start us, length us, event | category | flops | bytes accessed | tf_op | source)
XLA Modules:
  0.0 364.6 jit_solution(1658961827756413029)
XLA Ops:
  8.8 5.1 %convolution_convert_fusion.5 = bf16[1024,896]{1,0:T(8,128)(2,1)} fusion(bf16[1024,1024]{1,0:T(8,128)(2,1)S(1)} %copy-done, bf16[1024,896]{1,0:T(8,128)(2,1)} %param.17), kind=kOutput, calls=%fused_computation.13 | convolution fusion | flops 1879965696 | bytes 5767168 | tf_op jit(solution)/shard_map/dot_general | solution.py:107
  13.8 3.6 reshape_reshape.20
  17.4 5.1 %convolution_convert_fusion.4 = bf16[1024,896]{1,0:T(8,128)(2,1)} fusion(bf16[1024,1024]{1,0:T(8,128)(2,1)S(1)} %copy-done, bf16[1024,896]{1,0:T(8,128)(2,1)} %param.18), kind=kOutput, calls=%fused_computation.12 | convolution fusion | flops 1879965696 | bytes 5767168 | tf_op jit(solution)/shard_map/dot_general | solution.py:108
  22.5 3.7 %reshape_reshape.21 = bf16[8,114688]{1,0:T(8,128)(2,1)} reshape(bf16[1024,896]{1,0:T(8,128)(2,1)} %convolution_convert_fusion.4) | data formatting | bytes 3670016 | tf_op jit(solution)/shard_map/reshape;reshape | solution.py:21
  26.2 8.3 %pad_maximum_fusion = bf16[8,229376]{1,0:T(8,128)(2,1)} fusion(bf16[8,114688]{1,0:T(8,128)(2,1)} %reshape_reshape.21, bf16[8,114688]{1,0:T(8,128)(2,1)S(1)} %copy-done.3), kind=kLoop, calls=%fused_computation.5 | loop fusion | flops 7340032 | bytes 7340032 | tf_op jit(solution)/shard_map/concatenate | solution.py:21
  34.5 5.5 %reshape.88 = bf16[14336,128]{1,0:T(8,128)(2,1)} reshape(bf16[8,229376]{1,0:T(8,128)(2,1)} %pad_maximum_fusion) | data formatting | bytes 7340032 | tf_op jit(solution)/shard_map/reshape | solution.py:23
  40.1 37.3 %reduce-scatter.4.cloned.1.call-done = bf16[1792,128]{1,0:T(8,128)(2,1)} async-done(((bf16[14336,128]{1,0:T(8,128)(2,1)}), bf16[1792,128]{1,0:T(8,128)(2,1)}) %reduce-scatter.4.cloned.1.call-update) | async-done | bytes 458768 | tf_op jit(solution)/shard_map/reduce_scatter | solution.py:24
  79.9 4.9 %all-to-all-start.4 = ((bf16[4,128,896]{2,1,0:T(8,128)(2,1)}), bf16[4,128,896]{2,1,0:T(8,128)(2,1)S(1)}, u32[]{:S(2)}, u32[]{:S(2)}) async-start(bf16[4,128,896]{2,1,0:T(8,128)(2,1)} %broadcast_in_dim.16), calls=%async_computation.5 | async-start | bytes 1835008 | tf_op jit(solution)/shard_map/all_to_all | solution.py:34
  85.1 11.0 %all-to-all-done.4 = bf16[4,128,896]{2,1,0:T(8,128)(2,1)S(1)} async-done(((bf16[4,128,896]{2,1,0:T(8,128)(2,1)}), bf16[4,128,896]{2,1,0:T(8,128)(2,1)S(1)}, u32[]{:S(2)}, u32[]{:S(2)}) %all-to-all-start.4) | async-done | bytes 917536 | tf_op jit(solution)/shard_map/all_to_all | solution.py:34
  96.3 8.3 %all_to_all.111 = bf16[2,4,128,896]{3,2,1,0:T(8,128)(2,1)S(1)} all-to-all(bf16[2,4,128,896]{3,2,1,0:T(8,128)(2,1)S(1)} %broadcast_in_dim.17), channel_id=1, replica_groups=mesh['grp'=2,'wid_0'=4,'wid_1'=2,'hid_0'=2,'hid_1'=4] {'wid_1'}, dimensions={0} | all-to-all | bytes 3670016 | tf_op jit(solution)/shard_map/all_to_all | solution.py:34
  106.1 3.7 %convolution_convert_fusion.3 = bf16[1024,1024]{0,1:T(8,128)(2,1)} fusion(bf16[1024,896]{1,0:T(8,128)(2,1)S(1)} %bitcast.83, bf16[896,1024]{1,0:T(8,128)(2,1)S(1)} %copy-done.11), kind=kOutput, calls=%fused_computation.11 | convolution fusion | flops 1880096768 | bytes 5767168 | tf_op jit(solution)/shard_map/dot_general | solution.py:118
  116.9 23.1 %all_to_all.112 = bf16[8,2,8,4096]{3,2,1,0:T(8,128)(2,1)S(1)} all-to-all(bf16[8,2,8,4096]{3,2,1,0:T(8,128)(2,1)S(1)} %bitcast.78), channel_id=1, replica_groups=mesh['grp'=2,'wid_0'=4,'wid_1'=2,'hid_0'=2,'hid_1'=4] {'hid_0','hid_1'}, dimensions={0} | all-to-all | bytes 2097152 | tf_op jit(solution)/shard_map/all_to_all | solution.py:53
  140.2 8.4 %all_to_all.113 = bf16[2,8,4096]{2,1,0:T(8,128)(2,1)S(1)} all-to-all(bf16[2,8,4096]{2,1,0:T(8,128)(2,1)S(1)} %reduce_sum.85), channel_id=1, replica_groups=mesh['grp'=2,'wid_0'=4,'wid_1'=2,'hid_0'=2,'hid_1'=4] {'grp'}, dimensions={0} | all-to-all | bytes 262144 | tf_op jit(solution)/shard_map/all_to_all | solution.py:61
  148.6 7.3 %all_to_all.114 = bf16[2,8,4096]{2,1,0:T(8,128)(2,1)S(1)} all-to-all(bf16[2,8,4096]{2,1,0:T(8,128)(2,1)S(1)} %broadcast_in_dim.14), channel_id=1, replica_groups=mesh['grp'=2,'wid_0'=4,'wid_1'=2,'hid_0'=2,'hid_1'=4] {'grp'}, dimensions={0} | all-to-all | bytes 262144 | tf_op jit(solution)/shard_map/all_to_all | solution.py:34
  157.0 3.6 all-to-all-start.3
  160.7 15.1 %all-to-all-done.3 = bf16[8,2,8,4096]{3,2,1,0:T(8,128)(2,1)S(1)} async-done(((bf16[8,2,8,4096]{3,2,1,0:T(8,128)(2,1)}), bf16[8,2,8,4096]{3,2,1,0:T(8,128)(2,1)S(1)}, u32[]{:S(2)}, u32[]{:S(2)}) %all-to-all-start.3) | async-done | bytes 1048608 | tf_op jit(solution)/shard_map/all_to_all | solution.py:34
  177.3 13.6 %reduce-scatter.6.cloned.1.call-done = bf16[1024,64]{0,1:T(8,128)(2,1)} async-done(((bf16[1024,1024]{0,1:T(8,128)(2,1)}), bf16[1024,64]{0,1:T(8,128)(2,1)}) %reduce-scatter.6.cloned.1.call-update) | async-done | bytes 131088 | tf_op jit(solution)/shard_map/reduce_scatter | solution.py:122
  192.5 6.6 %all-to-all-start.6 = ((bf16[8,128,64]{1,2,0:T(8,128)(2,1)}), bf16[8,128,64]{1,2,0:T(8,128)(2,1)S(1)}, u32[]{:S(2)}, u32[]{:S(2)}) async-start(bf16[8,128,64]{1,2,0:T(8,128)(2,1)} %copy_bitcast_fusion.2), calls=%async_computation.8 | async-start | bytes 262144 | tf_op jit(solution)/shard_map/all_to_all | solution.py:128
  204.5 3.7 %fusion.3 = bf16[128,512]{1,0:T(8,128)(2,1)S(1)} fusion(f32[128,512]{1,0:T(8,128)S(1)} %copy.60, bf16[128,4096]{1,0:T(8,128)(2,1)S(1)} %fusion.1, bf16[4096,512]{0,1:T(8,128)(2,1)} %bitcast.69), kind=kOutput, calls=%fused_computation.18 | convolution fusion | flops 537067520 | bytes 5636096 | tf_op jit(solution)/shard_map/dot_general | solution.py:145
  212.1 18.1 %all_to_all.115 = bf16[8,2,8,4096]{3,2,1,0:T(8,128)(2,1)S(1)} all-to-all(bf16[8,2,8,4096]{3,2,1,0:T(8,128)(2,1)S(1)} %bitcast.79), channel_id=1, replica_groups=mesh['grp'=2,'wid_0'=4,'wid_1'=2,'hid_0'=2,'hid_1'=4] {'hid_0','hid_1'}, dimensions={0} | all-to-all | bytes 2097152 | tf_op jit(solution)/shard_map/all_to_all | solution.py:53
  230.3 7.7 %all_to_all.116 = bf16[2,8,4096]{2,1,0:T(8,128)(2,1)S(1)} all-to-all(bf16[2,8,4096]{2,1,0:T(8,128)(2,1)S(1)} %reduce_sum.87), channel_id=1, replica_groups=mesh['grp'=2,'wid_0'=4,'wid_1'=2,'hid_0'=2,'hid_1'=4] {'grp'}, dimensions={0} | all-to-all | bytes 262144 | tf_op jit(solution)/shard_map/all_to_all | solution.py:61
  238.1 7.2 %all_to_all.117 = bf16[2,8,4096]{2,1,0:T(8,128)(2,1)S(1)} all-to-all(bf16[2,8,4096]{2,1,0:T(8,128)(2,1)S(1)} %broadcast_in_dim.18), channel_id=1, replica_groups=mesh['grp'=2,'wid_0'=4,'wid_1'=2,'hid_0'=2,'hid_1'=4] {'grp'}, dimensions={0} | all-to-all | bytes 262144 | tf_op jit(solution)/shard_map/all_to_all | solution.py:34
  245.5 14.4 %all_to_all.118 = bf16[8,2,8,4096]{3,2,1,0:T(8,128)(2,1)S(1)} all-to-all(bf16[8,2,8,4096]{3,2,1,0:T(8,128)(2,1)S(1)} %broadcast_in_dim.19), channel_id=1, replica_groups=mesh['grp'=2,'wid_0'=4,'wid_1'=2,'hid_0'=2,'hid_1'=4] {'hid_0','hid_1'}, dimensions={0} | all-to-all | bytes 2097152 | tf_op jit(solution)/shard_map/all_to_all | solution.py:34
  261.2 5.1 %convolution_convert_fusion = bf16[4096,896]{1,0:T(8,128)(2,1)} fusion(bf16[128,448]{0,1:T(8,128)(2,1)S(1)} %get-tuple-element.38, bf16[128,448]{0,1:T(8,128)(2,1)S(1)} %get-tuple-element.37, bf16[128,4096]{1,0:T(8,128)(2,1)S(1)} %copy-done.2, f32[4096]{0:T(1024)S(1)} %copy-done.9, f32[128]{0:T(128)S(1)} %add_rsqrt_fusion), kind=kOutput, calls=%fused_computation | convolution fusion | flops 945750016 | bytes 8634880 | tf_op jit(solution)/shard_map/dot_general | solution.py:176
  271.3 4.4 %all-to-all-start.13 = ((bf16[16,128,256]{2,1,0:T(8,128)(2,1)}), bf16[16,128,256]{2,1,0:T(8,128)(2,1)}, u32[]{:S(2)}, u32[]{:S(2)}) async-start(bf16[16,128,256]{2,1,0:T(8,128)(2,1)} %bitcast.77), calls=%async_computation.16 | async-start | bytes 2097152 | tf_op jit(solution)/shard_map/all_to_all | solution.py:53
  277.0 12.0 %all-to-all-done.13 = bf16[16,128,256]{2,1,0:T(8,128)(2,1)} async-done(((bf16[16,128,256]{2,1,0:T(8,128)(2,1)}), bf16[16,128,256]{2,1,0:T(8,128)(2,1)}, u32[]{:S(2)}, u32[]{:S(2)}) %all-to-all-start.13) | async-done | bytes 1048608 | tf_op jit(solution)/shard_map/all_to_all | solution.py:53
  289.0 9.0 %all-to-all-start.12 = ((bf16[128,8,512]{0,2,1:T(8,128)(2,1)}), bf16[128,8,512]{0,2,1:T(8,128)(2,1)S(1)}, u32[]{:S(2)}, u32[]{:S(2)}) async-start(bf16[128,8,512]{0,2,1:T(8,128)(2,1)} %bitcast.76), calls=%async_computation.15 | async-start | bytes 2097152 | tf_op jit(solution)/shard_map/all_to_all | solution.py:171
  302.0 17.0 %all-to-all-done.12 = bf16[128,8,512]{0,2,1:T(8,128)(2,1)S(1)} async-done(((bf16[128,8,512]{0,2,1:T(8,128)(2,1)}), bf16[128,8,512]{0,2,1:T(8,128)(2,1)S(1)}, u32[]{:S(2)}, u32[]{:S(2)}) %all-to-all-start.12) | async-done | bytes 1048608 | tf_op jit(solution)/shard_map/all_to_all | solution.py:171
  319.6 3.5 all-to-all-start.14
  324.8 4.6 %all-to-all-done.14 = f32[16,128,1]{1,2,0:T(1,128)S(1)} async-done(((f32[16,128,1]{1,2,0:T(1,128)}), f32[16,128,1]{1,2,0:T(1,128)S(1)}, u32[]{:S(2)}, u32[]{:S(2)}) %all-to-all-start.14) | async-done | bytes 8224 | tf_op jit(solution)/shard_map/all_to_all | solution.py:34
  329.4 5.5 %all-to-all-start.11 = ((bf16[128,8,512]{2,0,1:T(8,128)(2,1)}), bf16[128,8,512]{2,0,1:T(8,128)(2,1)S(1)}, u32[]{:S(2)}, u32[]{:S(2)}) async-start(bf16[128,8,512]{2,0,1:T(8,128)(2,1)} %copy.64), calls=%async_computation.14 | async-start | bytes 2097152 | tf_op jit(solution)/shard_map/all_to_all | solution.py:172
  338.0 11.9 %all-to-all-done.11 = bf16[128,8,512]{2,0,1:T(8,128)(2,1)S(1)} async-done(((bf16[128,8,512]{2,0,1:T(8,128)(2,1)}), bf16[128,8,512]{2,0,1:T(8,128)(2,1)S(1)}, u32[]{:S(2)}, u32[]{:S(2)}) %all-to-all-start.11) | async-done | bytes 1048608 | tf_op jit(solution)/shard_map/all_to_all | solution.py:172
  (93 shorter events, 52.1 us)
Async XLA Ops:
  7.2 1.6 copy-start
  7.2 70.2 %reduce-scatter.4.cloned.1.call-start = ((), (), s32[]{:S(2)}) async-start(), calls=%async_computation.18 | async-start | bytes 4128768 | tf_op jit(solution)/shard_map/reduce_scatter | solution.py:24
  22.5 3.7 %copy-start.3 = (bf16[8,114688]{1,0:T(8,128)(2,1)S(1)}, bf16[8,114688]{1,0:T(8,128)(2,1)}, u32[]{:S(2)}) copy-start(bf16[8,114688]{1,0:T(8,128)(2,1)} %reshape_reshape.20) | copy-start | bytes 5505028
  78.7 6.1 %copy-start.2 = (bf16[128,4096]{1,0:T(8,128)(2,1)S(1)}, bf16[128,4096]{1,0:T(8,128)(2,1)}, u32[]{:S(2)}) copy-start(bf16[128,4096]{1,0:T(8,128)(2,1)} %param.10) | copy-start | bytes 3145732
  79.9 16.2 %all-to-all-start.4 = ((bf16[4,128,896]{2,1,0:T(8,128)(2,1)}), bf16[4,128,896]{2,1,0:T(8,128)(2,1)S(1)}, u32[]{:S(2)}, u32[]{:S(2)}) async-start(bf16[4,128,896]{2,1,0:T(8,128)(2,1)} %broadcast_in_dim.16), calls=%async_computation.5 | async-start | bytes 1835008 | tf_op jit(solution)/shard_map/all_to_all | solution.py:34
  84.8 106.1 %reduce-scatter.6.cloned.1.call-start = ((), (), s32[]{:S(2)}) async-start(), calls=%async_computation.19 | async-start | bytes 2228224 | tf_op jit(solution)/shard_map/reduce_scatter | solution.py:122
  104.6 1.5 copy-start.11
  109.8 0.7 copy-start.9
  110.5 3.4 copy-start.6
  113.9 1.9 copy-start.12
  113.9 2.1 copy-start.4
  157.0 18.8 %all-to-all-start.3 = ((bf16[8,2,8,4096]{3,2,1,0:T(8,128)(2,1)}), bf16[8,2,8,4096]{3,2,1,0:T(8,128)(2,1)S(1)}, u32[]{:S(2)}, u32[]{:S(2)}) async-start(bf16[8,2,8,4096]{3,2,1,0:T(8,128)(2,1)} %broadcast_in_dim.15), calls=%async_computation.3 | async-start | bytes 2097152 | tf_op jit(solution)/shard_map/all_to_all | solution.py:34
  192.5 11.8 %all-to-all-start.6 = ((bf16[8,128,64]{1,2,0:T(8,128)(2,1)}), bf16[8,128,64]{1,2,0:T(8,128)(2,1)S(1)}, u32[]{:S(2)}, u32[]{:S(2)}) async-start(bf16[8,128,64]{1,2,0:T(8,128)(2,1)} %copy_bitcast_fusion.2), calls=%async_computation.8 | async-start | bytes 262144 | tf_op jit(solution)/shard_map/all_to_all | solution.py:128
  199.1 150.9 %all-gather.2.cloned.1.call-start = ((), (), s32[]{:S(2)}) async-start(), calls=%async_computation.21 | async-start | bytes 2359296 | tf_op jit(solution)/shard_map/all_gather | solution.py:90
  209.0 145.6 %reduce-scatter.8.cloned.1.call-start = ((), (), s32[]{:S(2)}) async-start(), calls=%async_computation.20 | async-start | bytes 8257536 | tf_op jit(solution)/shard_map/reduce_scatter | solution.py:175
  245.4 14.6 %copy-start.5 = (bf16[448,4096]{1,0:T(8,128)(2,1)S(1)}, bf16[448,4096]{1,0:T(8,128)(2,1)}, u32[]{:S(2)}) copy-start(bf16[448,4096]{1,0:T(8,128)(2,1)} %param.14) | copy-start | bytes 11010052
  245.4 14.6 %copy-start.13 = (f32[128,448]{0,1:T(8,128)S(1)}, f32[128,448]{0,1:T(8,128)}, u32[]{:S(2)}) copy-start(f32[128,448]{0,1:T(8,128)} %copy-done.12) | copy-start | bytes 688132
  245.4 14.6 %copy-start.14 = (f32[128,448]{0,1:T(8,128)S(1)}, f32[128,448]{0,1:T(8,128)}, u32[]{:S(2)}) copy-start(f32[128,448]{0,1:T(8,128)} %get-tuple-element.42) | copy-start | bytes 688132
  266.3 3.1 copy-start.7
  271.3 17.7 %all-to-all-start.13 = ((bf16[16,128,256]{2,1,0:T(8,128)(2,1)}), bf16[16,128,256]{2,1,0:T(8,128)(2,1)}, u32[]{:S(2)}, u32[]{:S(2)}) async-start(bf16[16,128,256]{2,1,0:T(8,128)(2,1)} %bitcast.77), calls=%async_computation.16 | async-start | bytes 2097152 | tf_op jit(solution)/shard_map/all_to_all | solution.py:53
  289.0 30.0 %all-to-all-start.12 = ((bf16[128,8,512]{0,2,1:T(8,128)(2,1)}), bf16[128,8,512]{0,2,1:T(8,128)(2,1)S(1)}, u32[]{:S(2)}, u32[]{:S(2)}) async-start(bf16[128,8,512]{0,2,1:T(8,128)(2,1)} %bitcast.76), calls=%async_computation.15 | async-start | bytes 2097152 | tf_op jit(solution)/shard_map/all_to_all | solution.py:171
  319.6 9.8 %all-to-all-start.14 = ((f32[16,128,1]{1,2,0:T(1,128)}), f32[16,128,1]{1,2,0:T(1,128)S(1)}, u32[]{:S(2)}, u32[]{:S(2)}) async-start(f32[16,128,1]{1,2,0:T(1,128)} %broadcast_in_dim.20), calls=%async_computation.17 | async-start | bytes 16384 | tf_op jit(solution)/shard_map/all_to_all | solution.py:34
  329.4 20.5 %all-to-all-start.11 = ((bf16[128,8,512]{2,0,1:T(8,128)(2,1)}), bf16[128,8,512]{2,0,1:T(8,128)(2,1)S(1)}, u32[]{:S(2)}, u32[]{:S(2)}) async-start(bf16[128,8,512]{2,0,1:T(8,128)(2,1)} %copy.64), calls=%async_computation.14 | async-start | bytes 2097152 | tf_op jit(solution)/shard_map/all_to_all | solution.py:172
  338.0 14.8 %copy-start.8 = (bf16[8,128,512]{2,1,0:T(8,128)(2,1)S(1)}, bf16[8,128,512]{2,1,0:T(8,128)(2,1)}, u32[]{:S(2)}) copy-start(bf16[8,128,512]{2,1,0:T(8,128)(2,1)} %copy.66) | copy-start | bytes 3145732
  349.9 2.8 copy-start.10
  352.8 5.3 %copy-start.1 = (bf16[1024,1024]{1,0:T(8,128)(2,1)S(1)}, bf16[1024,1024]{1,0:T(8,128)(2,1)}, u32[]{:S(2)}) copy-start(bf16[1024,1024]{1,0:T(8,128)(2,1)} %param.16) | copy-start | bytes 6291460
Sparse Core Ops, SparseCore 0:
  40.2 37.1 reduce-scatter.3
  110.0 80.8 reduce-scatter.5
  209.2 23.2 all-gather.1
  266.4 57.8 reduce-scatter.7
where the time goes:
time: 366 us; the launch traced here: 365 us
  waiting for transfers between devices  126 us (34%)
  blocking collectives  94.6 us (26%)
  matrix products  41.1 us (11%)
  starting transfers between devices  37.5 us (10%)
  local copies, waits for them, and re-layouts  31.3 us (9%)
  other arithmetic  20 us (5%)
  between operations  14.1 us (4%)
    all_to_all x2, blocking collectives, sent_and_summed(): lax.all_to_all(blocks, axis, split_axis=0, concat_axis=0, tiled=True)  41.2 us
    reduce_scatter x1, waiting for transfers between devices, one_scatter(): lax.psum_scatter(lines, axis, tiled=True).reshape(-1)  37.3 us
    all_to_all x4, blocking collectives, from_everyone(): lax.all_to_all(jnp.broadcast_to(array[None], (peers, *array.shape)), axis...  37.2 us
    all_to_all x3, waiting for transfers between devices, from_everyone(): lax.all_to_all(jnp.broadcast_to(array[None], (peers, *array.shape)), axis...  30.7 us
    all_to_all x1, waiting for transfers between devices, shards(): lax.all_to_all(summed, WID, split_axis=1, concat_axis=0, tiled=True)  17 us
    all_to_all x2, blocking collectives, summed_rows(): lax.all_to_all(nearer.astype(jnp.bfloat16), far, split_axis=0, concat_axi...  16.1 us
    reduce_scatter x1, waiting for transfers between devices, shards(): lax.psum_scatter(feature_part.astype(jnp.bfloat16), GRP_HID, scatter_dime...  13.6 us
    all_to_all x1, waiting for transfers between devices, sent_and_summed(): lax.all_to_all(blocks, axis, split_axis=0, concat_axis=0, tiled=True)  12 us
  transfers between devices with their start and end apart: 11, of which 9 were waited for; matrix products, arithmetic and copies ran while one was open for 11% of the time, Pallas kernels for 0%

commit v1 on v0

--- a/solution.py
+++ b/solution.py
@@ -169,7 +169,15 @@
     paired_grad = jnp.concatenate([gate_grad, up_grad], axis=1)
     summed_cols, branch_cols = (
         lax.all_to_all(summed, WID, split_axis=1, concat_axis=0, tiled=True),
-        lax.all_to_all(branch_grad, WID, split_axis=1, concat_axis=0, tiled=True),
+        jnp.concatenate(
+            lax.all_to_all(
+                jnp.stack(jnp.split(branch_grad, lax.axis_size(WID), axis=1)),
+                concat_axis=0,
+                axis_name=WID,
+                split_axis=0,
+            ),
+            axis=0,
+        ),
     )
     hidden_all, error_all = in_one_piece((hidden, feature_error), WID, 0, 1)
     weight_grad = lax.psum_scatter(

time: 366 us -> 367 us (level)
  waiting for transfers between devices: 126 us -> 122 us
    all_to_all x1, waiting for transfers between devices: 12 us -> 7.75 us  [sent_and_summed(): lax.all_to_all(blocks, axis, split_axis=0, concat_axis=0, tiled=True)]
    unnamed x33 -> x39, local copies, waits for them, and re-layouts: 6.35 us -> 10.6 us
  transfers between devices with their start and end apart: 11 -> 11, of which waited for: 9 -> 9; matrix products, arithmetic and copies ran while one was open for 11% -> 12% of each run, Pallas kernels for 0% -> 0%
where the time goes in v1:
time: 367 us; the launch traced here: 366 us
  waiting for transfers between devices  122 us (33%)
  blocking collectives  94.6 us (26%)
  matrix products  41.5 us (11%)
  starting transfers between devices  38.2 us (10%)
  local copies, waits for them, and re-layouts  34.9 us (10%)
  other arithmetic  20 us (5%)
  between operations  14.1 us (4%)
    all_to_all x2, blocking collectives, sent_and_summed(): lax.all_to_all(blocks, axis, split_axis=0, concat_axis=0, tiled=True)  41.2 us
    reduce_scatter x1, waiting for transfers between devices, one_scatter(): lax.psum_scatter(lines, axis, tiled=True).reshape(-1)  37.3 us
    all_to_all x4, blocking collectives, from_everyone(): lax.all_to_all(jnp.broadcast_to(array[None], (peers, *array.shape)), axis...  37.2 us
    all_to_all x3, waiting for transfers between devices, from_everyone(): lax.all_to_all(jnp.broadcast_to(array[None], (peers, *array.shape)), axis...  31.7 us
    all_to_all x1, waiting for transfers between devices, shards(): lax.all_to_all(summed, WID, split_axis=1, concat_axis=0, tiled=True)  16.6 us
    all_to_all x2, blocking collectives, summed_rows(): lax.all_to_all(nearer.astype(jnp.bfloat16), far, split_axis=0, concat_axi...  16.1 us
    reduce_scatter x1, waiting for transfers between devices, shards(): lax.psum_scatter(feature_part.astype(jnp.bfloat16), GRP_HID, scatter_dime...  13.6 us
    all_to_all x1, waiting for transfers between devices, shards(): lax.all_to_all(jnp.stack(jnp.split(branch_grad, lax.axis_size(WID), axis=...  12 us
  transfers between devices with their start and end apart: 11, of which 9 were waited for; matrix products, arithmetic and copies ran while one was open for 12% of the time, Pallas kernels for 0%

profile of v1, /device:TPU:1, one launch (start us, length us, event | category | flops | bytes accessed | tf_op | source)
XLA Modules:
  0.0 365.7 jit_solution(3240365311254828148)
XLA Ops:
  8.8 5.1 %convolution_convert_fusion.5 = bf16[1024,896]{1,0:T(8,128)(2,1)} fusion(bf16[1024,1024]{1,0:T(8,128)(2,1)S(1)} %copy-done, bf16[1024,896]{1,0:T(8,128)(2,1)} %param.17), kind=kOutput, calls=%fused_computation.13 | convolution fusion | flops 1879965696 | bytes 5767168 | tf_op jit(solution)/shard_map/dot_general | solution.py:107
  13.8 3.6 reshape_reshape.20
  17.4 5.1 %convolution_convert_fusion.4 = bf16[1024,896]{1,0:T(8,128)(2,1)} fusion(bf16[1024,1024]{1,0:T(8,128)(2,1)S(1)} %copy-done, bf16[1024,896]{1,0:T(8,128)(2,1)} %param.18), kind=kOutput, calls=%fused_computation.12 | convolution fusion | flops 1879965696 | bytes 5767168 | tf_op jit(solution)/shard_map/dot_general | solution.py:108
  22.5 3.7 %reshape_reshape.21 = bf16[8,114688]{1,0:T(8,128)(2,1)} reshape(bf16[1024,896]{1,0:T(8,128)(2,1)} %convolution_convert_fusion.4) | data formatting | bytes 3670016 | tf_op jit(solution)/shard_map/reshape;reshape | solution.py:21
  26.2 8.3 %pad_maximum_fusion = bf16[8,229376]{1,0:T(8,128)(2,1)} fusion(bf16[8,114688]{1,0:T(8,128)(2,1)} %reshape_reshape.21, bf16[8,114688]{1,0:T(8,128)(2,1)S(1)} %copy-done.3), kind=kLoop, calls=%fused_computation.5 | loop fusion | flops 7340032 | bytes 7340032 | tf_op jit(solution)/shard_map/concatenate | solution.py:21
  34.5 5.5 %reshape.87 = bf16[14336,128]{1,0:T(8,128)(2,1)} reshape(bf16[8,229376]{1,0:T(8,128)(2,1)} %pad_maximum_fusion) | data formatting | bytes 7340032 | tf_op jit(solution)/shard_map/reshape | solution.py:23
  40.1 37.3 %reduce-scatter.4.cloned.1.call-done = bf16[1792,128]{1,0:T(8,128)(2,1)} async-done(((bf16[14336,128]{1,0:T(8,128)(2,1)}), bf16[1792,128]{1,0:T(8,128)(2,1)}) %reduce-scatter.4.cloned.1.call-update) | async-done | bytes 458768 | tf_op jit(solution)/shard_map/reduce_scatter | solution.py:24
  79.9 4.9 %all-to-all-start.4 = ((bf16[4,128,896]{2,1,0:T(8,128)(2,1)}), bf16[4,128,896]{2,1,0:T(8,128)(2,1)S(1)}, u32[]{:S(2)}, u32[]{:S(2)}) async-start(bf16[4,128,896]{2,1,0:T(8,128)(2,1)} %broadcast_in_dim.16), calls=%async_computation.5 | async-start | bytes 1835008 | tf_op jit(solution)/shard_map/all_to_all | solution.py:34
  85.1 11.0 %all-to-all-done.4 = bf16[4,128,896]{2,1,0:T(8,128)(2,1)S(1)} async-done(((bf16[4,128,896]{2,1,0:T(8,128)(2,1)}), bf16[4,128,896]{2,1,0:T(8,128)(2,1)S(1)}, u32[]{:S(2)}, u32[]{:S(2)}) %all-to-all-start.4) | async-done | bytes 917536 | tf_op jit(solution)/shard_map/all_to_all | solution.py:34
  96.3 8.3 %all_to_all.97 = bf16[2,4,128,896]{3,2,1,0:T(8,128)(2,1)S(1)} all-to-all(bf16[2,4,128,896]{3,2,1,0:T(8,128)(2,1)S(1)} %broadcast_in_dim.17), channel_id=1, replica_groups=mesh['grp'=2,'wid_0'=4,'wid_1'=2,'hid_0'=2,'hid_1'=4] {'wid_1'}, dimensions={0} | all-to-all | bytes 3670016 | tf_op jit(solution)/shard_map/all_to_all | solution.py:34
  106.1 3.7 %convolution_convert_fusion.3 = bf16[1024,1024]{0,1:T(8,128)(2,1)} fusion(bf16[1024,896]{1,0:T(8,128)(2,1)S(1)} %bitcast.115, bf16[896,1024]{1,0:T(8,128)(2,1)S(1)} %copy-done.11), kind=kOutput, calls=%fused_computation.11 | convolution fusion | flops 1880096768 | bytes 5767168 | tf_op jit(solution)/shard_map/dot_general | solution.py:118
  116.9 23.1 %all_to_all.98 = bf16[8,2,8,4096]{3,2,1,0:T(8,128)(2,1)S(1)} all-to-all(bf16[8,2,8,4096]{3,2,1,0:T(8,128)(2,1)S(1)} %bitcast.111), channel_id=1, replica_groups=mesh['grp'=2,'wid_0'=4,'wid_1'=2,'hid_0'=2,'hid_1'=4] {'hid_0','hid_1'}, dimensions={0} | all-to-all | bytes 2097152 | tf_op jit(solution)/shard_map/all_to_all | solution.py:53
  140.2 8.4 %all_to_all.99 = bf16[2,8,4096]{2,1,0:T(8,128)(2,1)S(1)} all-to-all(bf16[2,8,4096]{2,1,0:T(8,128)(2,1)S(1)} %reduce_sum.85), channel_id=1, replica_groups=mesh['grp'=2,'wid_0'=4,'wid_1'=2,'hid_0'=2,'hid_1'=4] {'grp'}, dimensions={0} | all-to-all | bytes 262144 | tf_op jit(solution)/shard_map/all_to_all | solution.py:61
  148.6 7.3 %all_to_all.100 = bf16[2,8,4096]{2,1,0:T(8,128)(2,1)S(1)} all-to-all(bf16[2,8,4096]{2,1,0:T(8,128)(2,1)S(1)} %broadcast_in_dim.14), channel_id=1, replica_groups=mesh['grp'=2,'wid_0'=4,'wid_1'=2,'hid_0'=2,'hid_1'=4] {'grp'}, dimensions={0} | all-to-all | bytes 262144 | tf_op jit(solution)/shard_map/all_to_all | solution.py:34
  157.0 3.6 all-to-all-start.3
  160.7 15.1 %all-to-all-done.3 = bf16[8,2,8,4096]{3,2,1,0:T(8,128)(2,1)S(1)} async-done(((bf16[8,2,8,4096]{3,2,1,0:T(8,128)(2,1)}), bf16[8,2,8,4096]{3,2,1,0:T(8,128)(2,1)S(1)}, u32[]{:S(2)}, u32[]{:S(2)}) %all-to-all-start.3) | async-done | bytes 1048608 | tf_op jit(solution)/shard_map/all_to_all | solution.py:34
  177.3 13.6 %reduce-scatter.6.cloned.1.call-done = bf16[1024,64]{0,1:T(8,128)(2,1)} async-done(((bf16[1024,1024]{0,1:T(8,128)(2,1)}), bf16[1024,64]{0,1:T(8,128)(2,1)}) %reduce-scatter.6.cloned.1.call-update) | async-done | bytes 131088 | tf_op jit(solution)/shard_map/reduce_scatter | solution.py:122
  192.5 6.6 %all-to-all-start.6 = ((bf16[8,128,64]{1,2,0:T(8,128)(2,1)}), bf16[8,128,64]{1,2,0:T(8,128)(2,1)S(1)}, u32[]{:S(2)}, u32[]{:S(2)}) async-start(bf16[8,128,64]{1,2,0:T(8,128)(2,1)} %copy_bitcast_fusion.2), calls=%async_computation.8 | async-start | bytes 262144 | tf_op jit(solution)/shard_map/all_to_all | solution.py:128
  204.5 3.7 %fusion.3 = bf16[128,512]{1,0:T(8,128)(2,1)S(1)} fusion(f32[128,512]{1,0:T(8,128)S(1)} %copy.56, bf16[128,4096]{1,0:T(8,128)(2,1)S(1)} %fusion.1, bf16[4096,512]{0,1:T(8,128)(2,1)} %bitcast.95), kind=kOutput, calls=%fused_computation.18 | convolution fusion | flops 537067520 | bytes 5636096 | tf_op jit(solution)/shard_map/dot_general | solution.py:145
  212.1 18.1 %all_to_all.101 = bf16[8,2,8,4096]{3,2,1,0:T(8,128)(2,1)S(1)} all-to-all(bf16[8,2,8,4096]{3,2,1,0:T(8,128)(2,1)S(1)} %bitcast.112), channel_id=1, replica_groups=mesh['grp'=2,'wid_0'=4,'wid_1'=2,'hid_0'=2,'hid_1'=4] {'hid_0','hid_1'}, dimensions={0} | all-to-all | bytes 2097152 | tf_op jit(solution)/shard_map/all_to_all | solution.py:53
  230.3 7.7 %all_to_all.102 = bf16[2,8,4096]{2,1,0:T(8,128)(2,1)S(1)} all-to-all(bf16[2,8,4096]{2,1,0:T(8,128)(2,1)S(1)} %reduce_sum.87), channel_id=1, replica_groups=mesh['grp'=2,'wid_0'=4,'wid_1'=2,'hid_0'=2,'hid_1'=4] {'grp'}, dimensions={0} | all-to-all | bytes 262144 | tf_op jit(solution)/shard_map/all_to_all | solution.py:61
  238.1 7.2 %all_to_all.103 = bf16[2,8,4096]{2,1,0:T(8,128)(2,1)S(1)} all-to-all(bf16[2,8,4096]{2,1,0:T(8,128)(2,1)S(1)} %broadcast_in_dim.18), channel_id=1, replica_groups=mesh['grp'=2,'wid_0'=4,'wid_1'=2,'hid_0'=2,'hid_1'=4] {'grp'}, dimensions={0} | all-to-all | bytes 262144 | tf_op jit(solution)/shard_map/all_to_all | solution.py:34
  245.5 14.4 %all_to_all.104 = bf16[8,2,8,4096]{3,2,1,0:T(8,128)(2,1)S(1)} all-to-all(bf16[8,2,8,4096]{3,2,1,0:T(8,128)(2,1)S(1)} %broadcast_in_dim.19), channel_id=1, replica_groups=mesh['grp'=2,'wid_0'=4,'wid_1'=2,'hid_0'=2,'hid_1'=4] {'hid_0','hid_1'}, dimensions={0} | all-to-all | bytes 2097152 | tf_op jit(solution)/shard_map/all_to_all | solution.py:34
  261.2 5.1 %convolution_convert_fusion = bf16[4096,896]{1,0:T(8,128)(2,1)} fusion(bf16[128,448]{0,1:T(8,128)(2,1)S(1)} %get-tuple-element.38, bf16[128,448]{0,1:T(8,128)(2,1)S(1)} %get-tuple-element.37, bf16[128,4096]{1,0:T(8,128)(2,1)S(1)} %copy-done.2, f32[4096]{0:T(1024)S(1)} %copy-done.9, f32[128]{0:T(128)S(1)} %add_rsqrt_fusion), kind=kOutput, calls=%fused_computation | convolution fusion | flops 945750016 | bytes 8634880 | tf_op jit(solution)/shard_map/dot_general | solution.py:184
  271.3 4.4 %all-to-all-start.13 = ((bf16[16,128,256]{2,1,0:T(8,128)(2,1)}), bf16[16,128,256]{2,1,0:T(8,128)(2,1)}, u32[]{:S(2)}, u32[]{:S(2)}) async-start(bf16[16,128,256]{2,1,0:T(8,128)(2,1)} %bitcast.108), calls=%async_computation.16 | async-start | bytes 2097152 | tf_op jit(solution)/shard_map/all_to_all | solution.py:53
  281.3 7.7 %all-to-all-done.13 = bf16[16,128,256]{2,1,0:T(8,128)(2,1)} async-done(((bf16[16,128,256]{2,1,0:T(8,128)(2,1)}), bf16[16,128,256]{2,1,0:T(8,128)(2,1)}, u32[]{:S(2)}, u32[]{:S(2)}) %all-to-all-start.13) | async-done | bytes 1048608 | tf_op jit(solution)/shard_map/all_to_all | solution.py:53
  289.0 9.0 %all-to-all-start.12 = ((bf16[128,8,512]{0,2,1:T(8,128)(2,1)}), bf16[128,8,512]{0,2,1:T(8,128)(2,1)S(1)}, u32[]{:S(2)}, u32[]{:S(2)}) async-start(bf16[128,8,512]{0,2,1:T(8,128)(2,1)} %bitcast.110), calls=%async_computation.15 | async-start | bytes 2097152 | tf_op jit(solution)/shard_map/all_to_all | solution.py:171
  302.5 16.6 %all-to-all-done.12 = bf16[128,8,512]{0,2,1:T(8,128)(2,1)S(1)} async-done(((bf16[128,8,512]{0,2,1:T(8,128)(2,1)}), bf16[128,8,512]{0,2,1:T(8,128)(2,1)S(1)}, u32[]{:S(2)}, u32[]{:S(2)}) %all-to-all-start.12) | async-done | bytes 1048608 | tf_op jit(solution)/shard_map/all_to_all | solution.py:171
  319.6 3.5 all-to-all-start.14
  323.8 5.6 %all-to-all-done.14 = f32[16,128,1]{1,2,0:T(1,128)S(1)} async-done(((f32[16,128,1]{1,2,0:T(1,128)}), f32[16,128,1]{1,2,0:T(1,128)S(1)}, u32[]{:S(2)}, u32[]{:S(2)}) %all-to-all-start.14) | async-done | bytes 8224 | tf_op jit(solution)/shard_map/all_to_all | solution.py:34
  329.4 6.2 %all-to-all-start.11 = ((bf16[8,128,512]{2,1,0:T(8,128)(2,1)}), bf16[8,128,512]{2,1,0:T(8,128)(2,1)}, u32[]{:S(2)}, u32[]{:S(2)}) async-start(bf16[8,128,512]{2,1,0:T(8,128)(2,1)} %fusion.9), calls=%async_computation.14 | async-start | bytes 2097152 | tf_op jit(solution)/shard_map/all_to_all | solution.py:173
  338.7 12.0 %all-to-all-done.11 = bf16[8,128,512]{2,1,0:T(8,128)(2,1)} async-done(((bf16[8,128,512]{2,1,0:T(8,128)(2,1)}), bf16[8,128,512]{2,1,0:T(8,128)(2,1)}, u32[]{:S(2)}, u32[]{:S(2)}) %all-to-all-start.11) | async-done | bytes 1048608 | tf_op jit(solution)/shard_map/all_to_all | solution.py:173
  (99 shorter events, 56.1 us)
Async XLA Ops:
  7.2 1.6 copy-start
  7.2 70.2 %reduce-scatter.4.cloned.1.call-start = ((), (), s32[]{:S(2)}) async-start(), calls=%async_computation.18 | async-start | bytes 4128768 | tf_op jit(solution)/shard_map/reduce_scatter | solution.py:24
  22.5 3.7 %copy-start.3 = (bf16[8,114688]{1,0:T(8,128)(2,1)S(1)}, bf16[8,114688]{1,0:T(8,128)(2,1)}, u32[]{:S(2)}) copy-start(bf16[8,114688]{1,0:T(8,128)(2,1)} %reshape_reshape.20) | copy-start | bytes 5505028
  78.7 6.1 %copy-start.2 = (bf16[128,4096]{1,0:T(8,128)(2,1)S(1)}, bf16[128,4096]{1,0:T(8,128)(2,1)}, u32[]{:S(2)}) copy-start(bf16[128,4096]{1,0:T(8,128)(2,1)} %param.10) | copy-start | bytes 3145732
  79.9 16.2 %all-to-all-start.4 = ((bf16[4,128,896]{2,1,0:T(8,128)(2,1)}), bf16[4,128,896]{2,1,0:T(8,128)(2,1)S(1)}, u32[]{:S(2)}, u32[]{:S(2)}) async-start(bf16[4,128,896]{2,1,0:T(8,128)(2,1)} %broadcast_in_dim.16), calls=%async_computation.5 | async-start | bytes 1835008 | tf_op jit(solution)/shard_map/all_to_all | solution.py:34
  84.8 106.1 %reduce-scatter.6.cloned.1.call-start = ((), (), s32[]{:S(2)}) async-start(), calls=%async_computation.19 | async-start | bytes 2228224 | tf_op jit(solution)/shard_map/reduce_scatter | solution.py:122
  104.6 1.5 copy-start.11
  109.8 0.7 copy-start.9
  110.5 3.4 copy-start.6
  113.9 1.9 copy-start.12
  113.9 2.1 copy-start.4
  157.0 18.8 %all-to-all-start.3 = ((bf16[8,2,8,4096]{3,2,1,0:T(8,128)(2,1)}), bf16[8,2,8,4096]{3,2,1,0:T(8,128)(2,1)S(1)}, u32[]{:S(2)}, u32[]{:S(2)}) async-start(bf16[8,2,8,4096]{3,2,1,0:T(8,128)(2,1)} %broadcast_in_dim.15), calls=%async_computation.3 | async-start | bytes 2097152 | tf_op jit(solution)/shard_map/all_to_all | solution.py:34
  192.5 11.8 %all-to-all-start.6 = ((bf16[8,128,64]{1,2,0:T(8,128)(2,1)}), bf16[8,128,64]{1,2,0:T(8,128)(2,1)S(1)}, u32[]{:S(2)}, u32[]{:S(2)}) async-start(bf16[8,128,64]{1,2,0:T(8,128)(2,1)} %copy_bitcast_fusion.2), calls=%async_computation.8 | async-start | bytes 262144 | tf_op jit(solution)/shard_map/all_to_all | solution.py:128
  199.1 151.6 %all-gather.2.cloned.1.call-start = ((), (), s32[]{:S(2)}) async-start(), calls=%async_computation.21 | async-start | bytes 2359296 | tf_op jit(solution)/shard_map/all_gather | solution.py:90
  209.0 146.7 %reduce-scatter.8.cloned.1.call-start = ((), (), s32[]{:S(2)}) async-start(), calls=%async_computation.20 | async-start | bytes 8257536 | tf_op jit(solution)/shard_map/reduce_scatter | solution.py:183
  245.4 14.6 %copy-start.5 = (bf16[448,4096]{1,0:T(8,128)(2,1)S(1)}, bf16[448,4096]{1,0:T(8,128)(2,1)}, u32[]{:S(2)}) copy-start(bf16[448,4096]{1,0:T(8,128)(2,1)} %param.14) | copy-start | bytes 11010052
  245.4 14.6 %copy-start.13 = (f32[128,448]{0,1:T(8,128)S(1)}, f32[128,448]{0,1:T(8,128)}, u32[]{:S(2)}) copy-start(f32[128,448]{0,1:T(8,128)} %copy-done.12) | copy-start | bytes 688132
  245.4 14.6 %copy-start.14 = (f32[128,448]{0,1:T(8,128)S(1)}, f32[128,448]{0,1:T(8,128)}, u32[]{:S(2)}) copy-start(f32[128,448]{0,1:T(8,128)} %get-tuple-element.42) | copy-start | bytes 688132
  266.3 3.1 copy-start.7
  271.3 17.7 %all-to-all-start.13 = ((bf16[16,128,256]{2,1,0:T(8,128)(2,1)}), bf16[16,128,256]{2,1,0:T(8,128)(2,1)}, u32[]{:S(2)}, u32[]{:S(2)}) async-start(bf16[16,128,256]{2,1,0:T(8,128)(2,1)} %bitcast.108), calls=%async_computation.16 | async-start | bytes 2097152 | tf_op jit(solution)/shard_map/all_to_all | solution.py:53
  289.0 30.0 %all-to-all-start.12 = ((bf16[128,8,512]{0,2,1:T(8,128)(2,1)}), bf16[128,8,512]{0,2,1:T(8,128)(2,1)S(1)}, u32[]{:S(2)}, u32[]{:S(2)}) async-start(bf16[128,8,512]{0,2,1:T(8,128)(2,1)} %bitcast.110), calls=%async_computation.15 | async-start | bytes 2097152 | tf_op jit(solution)/shard_map/all_to_all | solution.py:171
  319.6 9.8 %all-to-all-start.14 = ((f32[16,128,1]{1,2,0:T(1,128)}), f32[16,128,1]{1,2,0:T(1,128)S(1)}, u32[]{:S(2)}, u32[]{:S(2)}) async-start(f32[16,128,1]{1,2,0:T(1,128)} %broadcast_in_dim.20), calls=%async_computation.17 | async-start | bytes 16384 | tf_op jit(solution)/shard_map/all_to_all | solution.py:34
  329.4 21.3 %all-to-all-start.11 = ((bf16[8,128,512]{2,1,0:T(8,128)(2,1)}), bf16[8,128,512]{2,1,0:T(8,128)(2,1)}, u32[]{:S(2)}, u32[]{:S(2)}) async-start(bf16[8,128,512]{2,1,0:T(8,128)(2,1)} %fusion.9), calls=%async_computation.14 | async-start | bytes 2097152 | tf_op jit(solution)/shard_map/all_to_all | solution.py:173
  338.7 15.2 %copy-start.8 = (bf16[8,128,512]{2,1,0:T(8,128)(2,1)S(1)}, bf16[8,128,512]{2,1,0:T(8,128)(2,1)}, u32[]{:S(2)}) copy-start(bf16[8,128,512]{2,1,0:T(8,128)(2,1)} %copy.61) | copy-start | bytes 3145732
  350.7 3.1 copy-start.10
  353.8 5.3 %copy-start.1 = (bf16[1024,1024]{1,0:T(8,128)(2,1)S(1)}, bf16[1024,1024]{1,0:T(8,128)(2,1)}, u32[]{:S(2)}) copy-start(bf16[1024,1024]{1,0:T(8,128)(2,1)} %param.16) | copy-start | bytes 6291460
Sparse Core Ops, SparseCore 0:
  40.2 37.1 reduce-scatter.3
  110.0 80.8 reduce-scatter.5
  209.2 23.2 all-gather.1
  266.4 57.8 reduce-scatter.7
